TPU v7x, 512 devices: a whole 4x8x8 slice. The times are simulated.
512 devices in a mesh: row: 32 (over z_lo, y), col: 16 (over x, z_hi, core).
Axes of the slice: x: 4, y: 8, z: 8 (z_hi: 2, z_lo: 4; z = z_hi * 4 + z_lo), core: 2. Of those that a mesh axis runs over, the one named last changes fastest.
Arguments:
- queries: bfloat16 [1, 32, 32, 64, 2048], P(None, 'row', 'col'), may hold values from -17 to 17
- keys: bfloat16 [1, 32, 32, 64, 2048], P(None, 'row', 'col'), may hold values from -5.5 to 5.5
- values: bfloat16 [1, 32, 32, 64, 2048], P(None, 'row', 'col'), may hold values from -6 to 6
- pool_keys: bfloat16 [1024, 16, 2048], P(('row', 'col')), may hold values from -6 to 6
- pool_values: bfloat16 [1024, 16, 2048], P(('row', 'col')), may hold values from -6 to 6
- top_keys: bfloat16 [1, 128, 2048], P(None, 'col'), may hold values from -6 to 6
- top_values: bfloat16 [1, 128, 2048], P(None, 'col'), may hold values from -6 to 6
- coarse_ids: int32 [1, 32, 32, 8], P(None, 'row', 'col'), may hold values from 0 to 1023, as said below
Outputs:
- attended: bfloat16 [1, 32, 32, 64, 2048], P(None, 'row', 'col')
Inputs may be any that keep to these rules, and one draw needn't show every extreme that they name: Entry coarse_ids[n, i, j, c] names a pool block held by the device that holds fine block (i, j) or by one of its eight neighbours in the mesh (no wrap); the device with row index r and col index q holds pool blocks (r * 16 + q) * 2 to (r * 16 + q + 1) * 2 - 1. The 8 entries of a fine block differ.
All inputs are finite; a program needn't handle non-finite values.
Results may differ from a plain program's by a relative error of at most 0.0049.
Values may be sent and summed in bfloat16 or wider, within the bound.
No kernel may reach another device: no remote copies, remote signals or barrier semaphores. Data moves between devices by JAX's collectives and lax.ppermute only.
A program may use at most 64 MiB of HBM per device.

v0:
```python
import math
import jax
import jax.numpy as jnp
from jax import lax
from jax.sharding import PartitionSpec as P

HEADS = 16
NEG_FILL = -1e30


def extended(block, sides, width):
    for axis, dim in sides:
        count = lax.axis_size(axis)
        forward = [(i, i + 1) for i in range(count - 1)]
        backward = [(target, source) for source, target in forward]
        low = lax.ppermute(
            lax.slice_in_dim(block, block.shape[dim] - width, None, axis=dim), axis, forward
        )
        high = lax.ppermute(lax.slice_in_dim(block, 0, width, axis=dim), axis, backward)
        block = jnp.concatenate([low, block, high], axis=dim)
    return block


def body(queries, keys, values, pool_keys, pool_values, top_keys, top_values, coarse_ids):
    images, brow_count, bcol_count, block_tokens, model_width = queries.shape
    head_count = HEADS
    head_width = model_width // head_count
    score_scale = 1.0 / math.sqrt(head_width)
    pool_blocks = pool_keys.shape[0]
    pool_tokens = pool_keys.shape[1]
    row_count = lax.axis_size("row")
    col_count = lax.axis_size("col")
    row_index = lax.axis_index("row")
    col_index = lax.axis_index("col")
    pool_key_grid = pool_keys.reshape(1, 1, 1, pool_blocks * pool_tokens, model_width)
    pool_value_grid = pool_values.reshape(1, 1, 1, pool_blocks * pool_tokens, model_width)
    near_keys, near_values = (
        extended(keys, (("row", 1), ("col", 2)), 1),
        extended(values, (("row", 1), ("col", 2)), 1),
    )
    around_keys, around_values = (
        extended(pool_key_grid, (("row", 1), ("col", 2)), 1),
        extended(pool_value_grid, (("row", 1), ("col", 2)), 1),
    )
    around_keys = around_keys.reshape(9 * pool_blocks, pool_tokens, model_width)
    around_values = around_values.reshape(9 * pool_blocks, pool_tokens, model_width)
    top_all_keys, top_all_values = (
        lax.all_gather(top_keys, "col", axis=1, tiled=True),
        lax.all_gather(top_values, "col", axis=1, tiled=True),
    )
    owner_device = coarse_ids // pool_blocks
    owner_row = owner_device // col_count
    owner_col = owner_device % col_count
    local_slot = (
        (owner_row - row_index + 1) * 3 + (owner_col - col_index + 1)
    ) * pool_blocks + coarse_ids % pool_blocks
    global_row = row_index * brow_count + jnp.arange(brow_count, dtype=jnp.int32)
    global_col = col_index * bcol_count + jnp.arange(bcol_count, dtype=jnp.int32)
    total_rows = brow_count * row_count
    total_cols = bcol_count * col_count
    blocks = brow_count * bcol_count
    coarse_length = coarse_ids.shape[-1] * pool_tokens
    valid_parts = []
    for row_step in range(3):
        row_valid = (global_row + row_step - 1 >= 0) & (global_row + row_step - 1 < total_rows)
        for col_step in range(3):
            col_valid = (global_col + col_step - 1 >= 0) & (global_col + col_step - 1 < total_cols)
            part_valid = (row_valid[:, None] & col_valid[None, :]).reshape(blocks, 1)
            valid_parts.append(jnp.broadcast_to(part_valid, (blocks, block_tokens)))
    valid_parts.append(jnp.ones((blocks, coarse_length), dtype=bool))
    list_valid = jnp.concatenate(valid_parts, axis=1).reshape(blocks, 1, 1, -1)

    def attend_image(image_items):
        query_image, key_image, value_image, slot_image, top_key_image, top_value_image = (
            image_items
        )
        query_heads = query_image.reshape(blocks, block_tokens, head_count, head_width)
        key_lists = []
        value_lists = []
        for row_step in range(3):
            for col_step in range(3):
                key_lists.append(
                    key_image[
                        row_step : row_step + brow_count, col_step : col_step + bcol_count
                    ].reshape(blocks, block_tokens, model_width)
                )
                value_lists.append(
                    value_image[
                        row_step : row_step + brow_count, col_step : col_step + bcol_count
                    ].reshape(blocks, block_tokens, model_width)
                )
        key_lists.append(around_keys[slot_image].reshape(blocks, coarse_length, model_width))
        value_lists.append(around_values[slot_image].reshape(blocks, coarse_length, model_width))
        key_list = jnp.concatenate(key_lists, axis=1).reshape(blocks, -1, head_count, head_width)
        value_list = jnp.concatenate(value_lists, axis=1).reshape(
            blocks, -1, head_count, head_width
        )
        near_scores = (
            jnp.einsum("bqhd,bkhd->bhqk", query_heads, key_list, preferred_element_type=jnp.float32)
            * score_scale
        )
        near_scores = jnp.where(list_valid, near_scores, NEG_FILL)
        top_key_heads = top_key_image.reshape(-1, head_count, head_width)
        top_value_heads = top_value_image.reshape(-1, head_count, head_width)
        top_scores = (
            jnp.einsum(
                "bqhd,khd->bhqk", query_heads, top_key_heads, preferred_element_type=jnp.float32
            )
            * score_scale
        )
        row_peak = jnp.maximum(
            jnp.max(near_scores, axis=-1, keepdims=True),
            jnp.max(top_scores, axis=-1, keepdims=True),
        )
        near_exponent = jnp.exp(near_scores - row_peak)
        top_exponent = jnp.exp(top_scores - row_peak)
        row_total = jnp.sum(near_exponent, axis=-1, keepdims=True) + jnp.sum(
            top_exponent, axis=-1, keepdims=True
        )
        near_weights = (near_exponent / row_total).astype(jnp.bfloat16)
        top_weights = (top_exponent / row_total).astype(jnp.bfloat16)
        result = jnp.einsum(
            "bhqk,bkhd->bqhd", near_weights, value_list, preferred_element_type=jnp.float32
        )
        result = result + jnp.einsum(
            "bhqk,khd->bqhd", top_weights, top_value_heads, preferred_element_type=jnp.float32
        )
        return result.reshape(brow_count, bcol_count, block_tokens, model_width).astype(
            jnp.bfloat16
        )

    return lax.map(
        attend_image, (queries, near_keys, near_values, local_slot, top_all_keys, top_all_values)
    )


def solution(mesh):
    placed = (
        P(None, "row", "col", None, None),
        P(None, "row", "col", None, None),
        P(None, "row", "col", None, None),
        P(("row", "col"), None, None),
        P(("row", "col"), None, None),
        P(None, "col", None),
        P(None, "col", None),
        P(None, "row", "col", None),
    )
    return jax.shard_map(
        body,
        mesh=mesh,
        in_specs=placed,
        out_specs=P(None, "row", "col", None, None),
        check_vma=False,
    )
```

profile of v0, /device:TPU:6, one launch (start us, length us, event | category | flops | bytes accessed | tf_op | source)
XLA Modules:
  0.0 241.0 jit_solution(14862765426312695609)
XLA Ops:
  0.0 3.6 %collective-permute-start = (bf16[1,1,2,64,2048]{4,3,2,1,0:T(8,128)(2,1)}, bf16[1,1,2,64,2048]{4,3,2,1,0:T(8,128)(2,1)S(1)}, u32[]{:S(2)}, u32[]{:S(2)}) collective-permute-start(bf16[1,1,2,64,2048]{4,3,2,1,0:T(8,128)(2,1)} %param.10), channel_id=1, source_target_pairs={{0,16},{16,32},{32,48},{48,64},{64,80},{80,96},{96,112},{112,128},... | collective-permute-start | bytes 1572872 | tf_op jit(solution)/shard_map/ppermute | solution.py:16
  3.6 1.3 collective-permute-start.1
  4.9 1.3 collective-permute-start.5
  6.2 5.8 %collective-permute-start.4 = (bf16[1,1,1,32,2048]{4,3,2,1,0:T(8,128)(2,1)}, bf16[1,1,1,32,2048]{4,3,2,1,0:T(8,128)(2,1)}, u32[]{:S(2)}, u32[]{:S(2)}) collective-permute-start(bf16[1,1,1,32,2048]{4,3,2,1,0:T(8,128)(2,1)} %bitcast.215), channel_id=1, source_target_pairs={{0,16},{16,32},{32,48},{48,64},{64,80},{80,96},{96,112},{112,128},... | collective-permute-start | bytes 393224 | tf_op jit(solution)/shard_map/ppermute | solution.py:16
  12.1 1.3 collective-permute-start.13
  16.5 1.1 copy.119
  17.8 35.2 %all_gather.6 = bf16[1,128,2048]{2,1,0:T(8,128)(2,1)S(1)} all-gather(bf16[1,8,2048]{2,1,0:T(8,128)(2,1)} %param.13), channel_id=1, replica_groups=mesh['row'=32,'col'=16] {'col'}, dimensions={1}, use_global_device_ids=true | all-gather | bytes 557056 | tf_op jit(solution)/shard_map/all_gather | solution.py:48
  54.0 27.7 %all_gather.7 = bf16[1,128,2048]{2,1,0:T(8,128)(2,1)S(1)} all-gather(bf16[1,8,2048]{2,1,0:T(8,128)(2,1)} %param.14), channel_id=1, replica_groups=mesh['row'=32,'col'=16] {'col'}, dimensions={1}, use_global_device_ids=true | all-gather | bytes 557056 | tf_op jit(solution)/shard_map/all_gather | solution.py:49
  81.8 1.0 copy.102
  88.1 8.0 %collective-permute-start.12 = (bf16[1,1,1,32,2048]{4,3,2,1,0:T(8,128)(2,1)S(1)}, bf16[1,1,1,32,2048]{4,3,2,1,0:T(8,128)(2,1)S(1)}, u32[]{:S(2)}, u32[]{:S(2)}) collective-permute-start(bf16[1,1,1,32,2048]{4,3,2,1,0:T(8,128)(2,1)S(1)} %bitcast.219), channel_id=1, source_target_pairs={{0,16},{16,32},{32,48},{48,64},{64,80},{80,96},{96,112},{112,128},... | collective-permute-start | bytes 393224 | tf_op jit(solution)/shard_map/ppermute | solution.py:16
  96.1 3.7 %collective-permute-start.8 = (bf16[1,1,2,64,2048]{4,3,2,1,0:T(8,128)(2,1)}, bf16[1,1,2,64,2048]{4,3,2,1,0:T(8,128)(2,1)S(1)}, u32[]{:S(2)}, u32[]{:S(2)}) collective-permute-start(bf16[1,1,2,64,2048]{4,3,2,1,0:T(8,128)(2,1)} %param.9), channel_id=1, source_target_pairs={{0,16},{16,32},{32,48},{48,64},{64,80},{80,96},{96,112},{112,128},... | collective-permute-start | bytes 1572872 | tf_op jit(solution)/shard_map/ppermute | solution.py:16
  99.7 1.0 pad_maximum_fusion.3
  100.8 1.3 collective-permute-start.9
  102.1 8.1 %collective-permute-start.7 = (bf16[1,3,1,32,2048]{4,3,2,1,0:T(8,128)(2,1)S(1)}, bf16[1,3,1,32,2048]{4,3,2,1,0:T(8,128)(2,1)S(1)}, u32[]{:S(2)}, u32[]{:S(2)}) collective-permute-start(bf16[1,3,1,32,2048]{4,3,2,1,0:T(8,128)(2,1)S(1)} %pad_maximum_fusion.3), channel_id=1, source_target_pairs={{1,0},{2,1},{3,2},{4,3},{5,4},{6,5},{7,6},{8,7},{9,8},{10,9},{11,1... | collective-permute-start | bytes 1179656 | tf_op jit(solution)/shard_map/ppermute | solution.py:19
  110.2 0.8 pad_maximum_fusion.2
  111.0 0.8 copy-done.2
  111.7 1.9 collective-permute-start.6
  113.7 1.1 constant_dynamic-update-slice_fusion.5
  114.7 1.1 constant_dynamic-update-slice_fusion.4
  115.8 8.4 %collective-permute-start.15 = (bf16[1,3,1,32,2048]{4,3,2,1,0:T(8,128)(2,1)}, bf16[1,3,1,32,2048]{4,3,2,1,0:T(8,128)(2,1)}, u32[]{:S(2)}, u32[]{:S(2)}) collective-permute-start(bf16[1,3,1,32,2048]{4,3,2,1,0:T(8,128)(2,1)} %pad_maximum_fusion.2), channel_id=1, source_target_pairs={{1,0},{2,1},{3,2},{4,3},{5,4},{6,5},{7,6},{8,7},{9,8},{10,9},{11,1... | collective-permute-start | bytes 1179656 | tf_op jit(solution)/shard_map/ppermute | solution.py:19
  124.3 1.1 constant_dynamic-update-slice_fusion.3
  125.4 1.3 fusion.19
  126.7 1.9 collective-permute-start.14
  128.6 0.8 constant_dynamic-update-slice_fusion.2
  129.4 1.9 constant_dynamic-update-slice_fusion.1
  131.3 8.4 %collective-permute-start.3 = (bf16[1,3,1,64,2048]{4,3,2,1,0:T(8,128)(2,1)}, bf16[1,3,1,64,2048]{4,3,2,1,0:T(8,128)(2,1)}, u32[]{:S(2)}, u32[]{:S(2)}) collective-permute-start(bf16[1,3,1,64,2048]{4,3,2,1,0:T(8,128)(2,1)} %get-tuple-element.59), channel_id=1, source_target_pairs={{1,0},{2,1},{3,2},{4,3},{5,4},{6,5},{7,6},{8,7},{9,8},{10,9},{11,1... | collective-permute-start | bytes 2359304 | tf_op jit(solution)/shard_map/ppermute | solution.py:19
  139.8 1.9 collective-permute-start.2
  141.7 2.1 pad_maximum_fusion.1
  143.8 0.9 constant_dynamic-update-slice_fusion
  144.7 3.0 %gather_fusion = bf16[16,16,2048]{2,1,0:T(8,128)(2,1)} fusion(bf16[18,16,2048]{2,1,0:T(8,128)(2,1)} %bitcast.168, s32[1024]{0:T(1024)} %pad_clamp_fusion), kind=kCustom, calls=%fused_computation | custom fusion | bytes 2097216 | tf_op jit(solution)/shard_map/while/body/eval_jaxpr/gather | solution.py:93
  147.7 2.4 %copy.129 = bf16[32,8,16,128]{3,2,1,0:T(8,128)(2,1)} copy(bf16[32,8,16,128]{3,1,2,0:T(8,128)(2,1)} %bitcast.173) | data formatting | bytes 2097152
  150.1 2.7 %fusion.18 = (bf16[1,3,1,64,2048]{4,3,2,1,0:T(8,128)(2,1)}, bf16[1,3,1,64,2048]{4,3,2,1,0:T(8,128)(2,1)}) fusion(bf16[1,3,2,64,2048]{4,3,2,1,0:T(8,128)(2,1)} %constant_dynamic-update-slice_fusion), kind=kLoop, calls=%fused_computation.87 | loop fusion | bytes 3145728 | tf_op jit(solution)/shard_map/slice | solution.py:17
  152.8 8.4 %collective-permute-start.11 = (bf16[1,3,1,64,2048]{4,3,2,1,0:T(8,128)(2,1)}, bf16[1,3,1,64,2048]{4,3,2,1,0:T(8,128)(2,1)}, u32[]{:S(2)}, u32[]{:S(2)}) collective-permute-start(bf16[1,3,1,64,2048]{4,3,2,1,0:T(8,128)(2,1)} %get-tuple-element.57), channel_id=1, source_target_pairs={{1,0},{2,1},{3,2},{4,3},{5,4},{6,5},{7,6},{8,7},{9,8},{10,9},{11,1... | collective-permute-start | bytes 2359304 | tf_op jit(solution)/shard_map/ppermute | solution.py:19
  161.3 1.9 collective-permute-start.10
  163.2 2.3 pad_maximum_fusion
  165.6 3.0 %gather_fusion.1 = bf16[16,16,2048]{2,1,0:T(8,128)(2,1)} fusion(bf16[18,16,2048]{2,1,0:T(8,128)(2,1)} %bitcast.169, s32[1024]{0:T(1024)} %pad_clamp_fusion), kind=kCustom, calls=%fused_computation.1 | custom fusion | bytes 2097216 | tf_op jit(solution)/shard_map/while/body/eval_jaxpr/gather | solution.py:92
  168.5 1.5 copy.118
  170.0 39.1 %collective-permute-done.2 = bf16[1,3,1,64,2048]{4,3,2,1,0:T(8,128)(2,1)} collective-permute-done((bf16[1,3,1,64,2048]{4,3,2,1,0:T(8,128)(2,1)}, bf16[1,3,1,64,2048]{4,3,2,1,0:T(8,128)(2,1)}, u32[]{:S(2)}, u32[]{:S(2)}) %collective-permute-start.2) | collective-permute-done | bytes 786464 | tf_op jit(solution)/shard_map/ppermute | solution.py:16
  209.1 1.7 maximum_bitcast_fusion.1
  210.9 0.8 fusion.17
  212.9 10.7 %collective-permute-done.10 = bf16[1,3,1,64,2048]{4,3,2,1,0:T(8,128)(2,1)} collective-permute-done((bf16[1,3,1,64,2048]{4,3,2,1,0:T(8,128)(2,1)}, bf16[1,3,1,64,2048]{4,3,2,1,0:T(8,128)(2,1)}, u32[]{:S(2)}, u32[]{:S(2)}) %collective-permute-start.10) | collective-permute-done | bytes 786464 | tf_op jit(solution)/shard_map/ppermute | solution.py:16
  223.6 2.2 maximum_bitcast_fusion
  225.8 0.8 fusion.16
  229.6 2.3 bitcast_reduce_fusion
  232.0 1.9 fusion.1
  236.4 2.2 fusion.4
  238.6 1.0 fusion.6
  240.0 1.0 convert_element_type.27
  (94 shorter events, 16.4 us)
Async XLA Ops:
  0.0 99.7 %copy-start.3 = (bf16[2,16,2048]{2,1,0:T(8,128)(2,1)S(1)}, bf16[2,16,2048]{2,1,0:T(8,128)(2,1)}, u32[]{:S(2)}) copy-start(bf16[2,16,2048]{2,1,0:T(8,128)(2,1)} %param.12) | copy-start | bytes 393220
  0.0 88.1 %copy-start.4 = (bf16[2,16,2048]{2,1,0:T(8,128)(2,1)S(1)}, bf16[2,16,2048]{2,1,0:T(8,128)(2,1)}, u32[]{:S(2)}) copy-start(bf16[2,16,2048]{2,1,0:T(8,128)(2,1)} %param.11) | copy-start | bytes 393220
  0.0 110.9 %collective-permute-start = (bf16[1,1,2,64,2048]{4,3,2,1,0:T(8,128)(2,1)}, bf16[1,1,2,64,2048]{4,3,2,1,0:T(8,128)(2,1)S(1)}, u32[]{:S(2)}, u32[]{:S(2)}) collective-permute-start(bf16[1,1,2,64,2048]{4,3,2,1,0:T(8,128)(2,1)} %param.10), channel_id=1, source_target_pairs={{0,16},{16,32},{32,48},{48,64},{64,80},{80,96},{96,112},{112,128},... | collective-permute-start | bytes 1572872 | tf_op jit(solution)/shard_map/ppermute | solution.py:16
  3.6 112.2 %collective-permute-start.1 = (bf16[1,1,2,64,2048]{4,3,2,1,0:T(8,128)(2,1)}, bf16[1,1,2,64,2048]{4,3,2,1,0:T(8,128)(2,1)}, u32[]{:S(2)}, u32[]{:S(2)}) collective-permute-start(bf16[1,1,2,64,2048]{4,3,2,1,0:T(8,128)(2,1)} %param.10), channel_id=1, source_target_pairs={{16,0},{32,16},{48,32},{64,48},{80,64},{96,80},{112,96},{128,112},... | collective-permute-start | bytes 1572872 | tf_op jit(solution)/shard_map/ppermute | solution.py:19
  4.9 83.1 %collective-permute-start.5 = (bf16[1,1,1,32,2048]{4,3,2,1,0:T(8,128)(2,1)}, bf16[1,1,1,32,2048]{4,3,2,1,0:T(8,128)(2,1)}, u32[]{:S(2)}, u32[]{:S(2)}) collective-permute-start(bf16[1,1,1,32,2048]{4,3,2,1,0:T(8,128)(2,1)} %bitcast.214), channel_id=1, source_target_pairs={{16,0},{32,16},{48,32},{64,48},{80,64},{96,80},{112,96},{128,112},... | collective-permute-start | bytes 393224 | tf_op jit(solution)/shard_map/ppermute | solution.py:19
  6.2 89.8 %collective-permute-start.4 = (bf16[1,1,1,32,2048]{4,3,2,1,0:T(8,128)(2,1)}, bf16[1,1,1,32,2048]{4,3,2,1,0:T(8,128)(2,1)}, u32[]{:S(2)}, u32[]{:S(2)}) collective-permute-start(bf16[1,1,1,32,2048]{4,3,2,1,0:T(8,128)(2,1)} %bitcast.215), channel_id=1, source_target_pairs={{0,16},{16,32},{32,48},{48,64},{64,80},{80,96},{96,112},{112,128},... | collective-permute-start | bytes 393224 | tf_op jit(solution)/shard_map/ppermute | solution.py:16
  12.1 88.7 %collective-permute-start.13 = (bf16[1,1,1,32,2048]{4,3,2,1,0:T(8,128)(2,1)}, bf16[1,1,1,32,2048]{4,3,2,1,0:T(8,128)(2,1)S(1)}, u32[]{:S(2)}, u32[]{:S(2)}) collective-permute-start(bf16[1,1,1,32,2048]{4,3,2,1,0:T(8,128)(2,1)} %bitcast.218), channel_id=1, source_target_pairs={{16,0},{32,16},{48,32},{64,48},{80,64},{96,80},{112,96},{128,112},... | collective-permute-start | bytes 393224 | tf_op jit(solution)/shard_map/ppermute | solution.py:19
  88.1 14.0 %collective-permute-start.12 = (bf16[1,1,1,32,2048]{4,3,2,1,0:T(8,128)(2,1)S(1)}, bf16[1,1,1,32,2048]{4,3,2,1,0:T(8,128)(2,1)S(1)}, u32[]{:S(2)}, u32[]{:S(2)}) collective-permute-start(bf16[1,1,1,32,2048]{4,3,2,1,0:T(8,128)(2,1)S(1)} %bitcast.219), channel_id=1, source_target_pairs={{0,16},{16,32},{32,48},{48,64},{64,80},{80,96},{96,112},{112,128},... | collective-permute-start | bytes 393224 | tf_op jit(solution)/shard_map/ppermute | solution.py:16
  96.1 30.6 %collective-permute-start.8 = (bf16[1,1,2,64,2048]{4,3,2,1,0:T(8,128)(2,1)}, bf16[1,1,2,64,2048]{4,3,2,1,0:T(8,128)(2,1)S(1)}, u32[]{:S(2)}, u32[]{:S(2)}) collective-permute-start(bf16[1,1,2,64,2048]{4,3,2,1,0:T(8,128)(2,1)} %param.9), channel_id=1, source_target_pairs={{0,16},{16,32},{32,48},{48,64},{64,80},{80,96},{96,112},{112,128},... | collective-permute-start | bytes 1572872 | tf_op jit(solution)/shard_map/ppermute | solution.py:16
  100.8 43.1 %collective-permute-start.9 = (bf16[1,1,2,64,2048]{4,3,2,1,0:T(8,128)(2,1)}, bf16[1,1,2,64,2048]{4,3,2,1,0:T(8,128)(2,1)S(1)}, u32[]{:S(2)}, u32[]{:S(2)}) collective-permute-start(bf16[1,1,2,64,2048]{4,3,2,1,0:T(8,128)(2,1)} %param.9), channel_id=1, source_target_pairs={{16,0},{32,16},{48,32},{64,48},{80,64},{96,80},{112,96},{128,112},... | collective-permute-start | bytes 1572872 | tf_op jit(solution)/shard_map/ppermute | solution.py:19
  102.1 13.8 %copy-start.5 = (bf16[1,1,1,32,2048]{4,3,2,1,0:T(8,128)(2,1)}, bf16[1,1,1,32,2048]{4,3,2,1,0:T(8,128)(2,1)S(1)}, u32[]{:S(2)}) copy-start(bf16[1,1,1,32,2048]{4,3,2,1,0:T(8,128)(2,1)S(1)} %collective-permute-done.12) | copy-start | bytes 393220
  102.1 29.2 %collective-permute-start.7 = (bf16[1,3,1,32,2048]{4,3,2,1,0:T(8,128)(2,1)S(1)}, bf16[1,3,1,32,2048]{4,3,2,1,0:T(8,128)(2,1)S(1)}, u32[]{:S(2)}, u32[]{:S(2)}) collective-permute-start(bf16[1,3,1,32,2048]{4,3,2,1,0:T(8,128)(2,1)S(1)} %pad_maximum_fusion.3), channel_id=1, source_target_pairs={{1,0},{2,1},{3,2},{4,3},{5,4},{6,5},{7,6},{8,7},{9,8},{10,9},{11,1... | collective-permute-start | bytes 1179656 | tf_op jit(solution)/shard_map/ppermute | solution.py:19
  110.9 0.8 copy-start.2
  111.7 28.0 %collective-permute-start.6 = (bf16[1,3,1,32,2048]{4,3,2,1,0:T(8,128)(2,1)S(1)}, bf16[1,3,1,32,2048]{4,3,2,1,0:T(8,128)(2,1)S(1)}, u32[]{:S(2)}, u32[]{:S(2)}) collective-permute-start(bf16[1,3,1,32,2048]{4,3,2,1,0:T(8,128)(2,1)S(1)} %pad_maximum_fusion.3), channel_id=1, source_target_pairs={{0,1},{1,2},{2,3},{3,4},{4,5},{5,6},{6,7},{7,8},{8,9},{9,10},{10,1... | collective-permute-start | bytes 1179656 | tf_op jit(solution)/shard_map/ppermute | solution.py:16
  115.8 45.4 %collective-permute-start.15 = (bf16[1,3,1,32,2048]{4,3,2,1,0:T(8,128)(2,1)}, bf16[1,3,1,32,2048]{4,3,2,1,0:T(8,128)(2,1)}, u32[]{:S(2)}, u32[]{:S(2)}) collective-permute-start(bf16[1,3,1,32,2048]{4,3,2,1,0:T(8,128)(2,1)} %pad_maximum_fusion.2), channel_id=1, source_target_pairs={{1,0},{2,1},{3,2},{4,3},{5,4},{6,5},{7,6},{8,7},{9,8},{10,9},{11,1... | collective-permute-start | bytes 1179656 | tf_op jit(solution)/shard_map/ppermute | solution.py:19
  126.7 36.5 %collective-permute-start.14 = (bf16[1,3,1,32,2048]{4,3,2,1,0:T(8,128)(2,1)}, bf16[1,3,1,32,2048]{4,3,2,1,0:T(8,128)(2,1)}, u32[]{:S(2)}, u32[]{:S(2)}) collective-permute-start(bf16[1,3,1,32,2048]{4,3,2,1,0:T(8,128)(2,1)} %pad_maximum_fusion.2), channel_id=1, source_target_pairs={{0,1},{1,2},{2,3},{3,4},{4,5},{5,6},{6,7},{7,8},{8,9},{9,10},{10,1... | collective-permute-start | bytes 1179656 | tf_op jit(solution)/shard_map/ppermute | solution.py:16
  131.3 38.7 %collective-permute-start.3 = (bf16[1,3,1,64,2048]{4,3,2,1,0:T(8,128)(2,1)}, bf16[1,3,1,64,2048]{4,3,2,1,0:T(8,128)(2,1)}, u32[]{:S(2)}, u32[]{:S(2)}) collective-permute-start(bf16[1,3,1,64,2048]{4,3,2,1,0:T(8,128)(2,1)} %get-tuple-element.59), channel_id=1, source_target_pairs={{1,0},{2,1},{3,2},{4,3},{5,4},{6,5},{7,6},{8,7},{9,8},{10,9},{11,1... | collective-permute-start | bytes 2359304 | tf_op jit(solution)/shard_map/ppermute | solution.py:19
  139.8 69.3 %collective-permute-start.2 = (bf16[1,3,1,64,2048]{4,3,2,1,0:T(8,128)(2,1)}, bf16[1,3,1,64,2048]{4,3,2,1,0:T(8,128)(2,1)}, u32[]{:S(2)}, u32[]{:S(2)}) collective-permute-start(bf16[1,3,1,64,2048]{4,3,2,1,0:T(8,128)(2,1)} %get-tuple-element.58), channel_id=1, source_target_pairs={{0,1},{1,2},{2,3},{3,4},{4,5},{5,6},{6,7},{7,8},{8,9},{9,10},{10,1... | collective-permute-start | bytes 2359304 | tf_op jit(solution)/shard_map/ppermute | solution.py:16
  152.8 60.1 %collective-permute-start.11 = (bf16[1,3,1,64,2048]{4,3,2,1,0:T(8,128)(2,1)}, bf16[1,3,1,64,2048]{4,3,2,1,0:T(8,128)(2,1)}, u32[]{:S(2)}, u32[]{:S(2)}) collective-permute-start(bf16[1,3,1,64,2048]{4,3,2,1,0:T(8,128)(2,1)} %get-tuple-element.57), channel_id=1, source_target_pairs={{1,0},{2,1},{3,2},{4,3},{5,4},{6,5},{7,6},{8,7},{9,8},{10,9},{11,1... | collective-permute-start | bytes 2359304 | tf_op jit(solution)/shard_map/ppermute | solution.py:19
  161.3 62.3 %collective-permute-start.10 = (bf16[1,3,1,64,2048]{4,3,2,1,0:T(8,128)(2,1)}, bf16[1,3,1,64,2048]{4,3,2,1,0:T(8,128)(2,1)}, u32[]{:S(2)}, u32[]{:S(2)}) collective-permute-start(bf16[1,3,1,64,2048]{4,3,2,1,0:T(8,128)(2,1)} %get-tuple-element.56), channel_id=1, source_target_pairs={{0,1},{1,2},{2,3},{3,4},{4,5},{5,6},{6,7},{7,8},{8,9},{9,10},{10,1... | collective-permute-start | bytes 2359304 | tf_op jit(solution)/shard_map/ppermute | solution.py:16
  227.7 1.9 copy-start.6
  233.9 2.2 copy-start
  236.4 2.2 copy-start.1
where the time goes:
time: 242 us; the launch traced here: 241 us
  starting transfers between devices  67.3 us (28%)
  blocking collectives  63 us (26%)
  waiting for transfers between devices  49.9 us (21%)
  local copies, waits for them, and re-layouts  38.1 us (16%)
  other arithmetic  16.2 us (7%)
  matrix products  5.78 us (2%)
    ppermute x8, waiting for transfers between devices, extended(): lax.ppermute(lax.slice_in_dim(block, block.shape[dim] - width, None, axis...  49.9 us
    ppermute x8, starting transfers between devices, extended(): lax.ppermute(lax.slice_in_dim(block, 0, width, axis=dim), axis, backward)  38.5 us
    all_gather x1, blocking collectives, body(): lax.all_gather(top_keys, 'col', axis=1, tiled=True)  35.2 us
    ppermute x8, starting transfers between devices, extended(): lax.ppermute(lax.slice_in_dim(block, block.shape[dim] - width, None, axis...  28.8 us
    all_gather x1, blocking collectives, body(): lax.all_gather(top_values, 'col', axis=1, tiled=True)  27.7 us
    unnamed x57, local copies, waits for them, and re-layouts  15.8 us
    concatenate x4, other arithmetic, extended(): block = jnp.concatenate([low, block, high], axis=dim)  6.27 us
  transfers between devices with their start and end apart: 16, of which 2 were waited for; matrix products, arithmetic and copies ran while one was open for 18% of the time, Pallas kernels for 0%

commit v1 on v0

--- a/solution.py
+++ b/solution.py
@@ -45,7 +45,9 @@
     around_keys = around_keys.reshape(9 * pool_blocks, pool_tokens, model_width)
     around_values = around_values.reshape(9 * pool_blocks, pool_tokens, model_width)
     top_all_keys, top_all_values = (
-        lax.all_gather(top_keys, "col", axis=1, tiled=True),
+        jnp.concatenate(
+            lax.all_to_all(jnp.stack([top_keys] * lax.axis_size("col")), "col", 0, 0), axis=1
+        ),
         lax.all_gather(top_values, "col", axis=1, tiled=True),
     )
     owner_device = coarse_ids // pool_blocks

time: 242 us -> 222 us (0.917)
  the two profiles are of different devices: /device:TPU:6 before, /device:TPU:4 now
where the time goes in v1:
time: 222 us; the launch traced here: 221 us
  starting transfers between devices  77 us (35%)
  waiting for transfers between devices  56.1 us (25%)
  blocking collectives  34.8 us (16%)
  local copies, waits for them, and re-layouts  32.5 us (15%)
  other arithmetic  12.4 us (6%)
  matrix products  7.01 us (3%)
    ppermute x8, starting transfers between devices, extended(): lax.ppermute(lax.slice_in_dim(block, 0, width, axis=dim), axis, backward)  36.7 us
    all_gather x1, blocking collectives, body(): lax.all_gather(top_values, 'col', axis=1, tiled=True)  34.8 us
    ppermute x8, waiting for transfers between devices, extended(): lax.ppermute(lax.slice_in_dim(block, block.shape[dim] - width, None, axis...  32.3 us
    ppermute x8, starting transfers between devices, extended(): lax.ppermute(lax.slice_in_dim(block, block.shape[dim] - width, None, axis...  27 us
    ppermute x8, waiting for transfers between devices, extended(): lax.ppermute(lax.slice_in_dim(block, 0, width, axis=dim), axis, backward)  23.8 us
    unnamed x70, local copies, waits for them, and re-layouts  15.1 us
    all_to_all x1, starting transfers between devices, body(): lax.all_to_all(jnp.stack([top_keys] * lax.axis_size('col')), 'col', 0, 0)  13.3 us
    concatenate x4, other arithmetic, extended(): block = jnp.concatenate([low, block, high], axis=dim)  5.24 us
  transfers between devices with their start and end apart: 17, of which 6 were waited for; matrix products, arithmetic and copies ran while one was open for 16% of the time, Pallas kernels for 0%

profile of v1, /device:TPU:4, one launch (start us, length us, event | category | flops | bytes accessed | tf_op | source)
XLA Modules:
  0.0 220.6 jit_solution(2684121386810606569)
XLA Ops:
  0.0 3.6 %collective-permute-start = (bf16[1,1,2,64,2048]{4,3,2,1,0:T(8,128)(2,1)}, bf16[1,1,2,64,2048]{4,3,2,1,0:T(8,128)(2,1)S(1)}, u32[]{:S(2)}, u32[]{:S(2)}) collective-permute-start(bf16[1,1,2,64,2048]{4,3,2,1,0:T(8,128)(2,1)} %param.10), channel_id=1, source_target_pairs={{0,16},{16,32},{32,48},{48,64},{64,80},{80,96},{96,112},{112,128},... | collective-permute-start | bytes 1572872 | tf_op jit(solution)/shard_map/ppermute | solution.py:16
  3.6 1.3 collective-permute-start.1
  4.9 1.3 collective-permute-start.5
  6.2 5.2 %collective-permute-start.4 = (bf16[1,1,1,32,2048]{4,3,2,1,0:T(8,128)(2,1)}, bf16[1,1,1,32,2048]{4,3,2,1,0:T(8,128)(2,1)S(1)}, u32[]{:S(2)}, u32[]{:S(2)}) collective-permute-start(bf16[1,1,1,32,2048]{4,3,2,1,0:T(8,128)(2,1)} %bitcast.218), channel_id=1, source_target_pairs={{0,16},{16,32},{32,48},{48,64},{64,80},{80,96},{96,112},{112,128},... | collective-permute-start | bytes 393224 | tf_op jit(solution)/shard_map/ppermute | solution.py:16
  11.4 1.3 collective-permute-start.13
  12.7 1.7 stack.2
  14.4 13.3 %all-to-all-start = ((bf16[16,1,8,2048]{3,2,1,0:T(8,128)(2,1)}), bf16[16,1,8,2048]{3,2,1,0:T(8,128)(2,1)}, u32[]{:S(2)}, u32[]{:S(2)}) async-start(bf16[16,1,8,2048]{3,2,1,0:T(8,128)(2,1)} %stack.2), calls=%async_computation | async-start | bytes 1048576 | tf_op jit(solution)/shard_map/all_to_all | solution.py:49
  28.5 34.8 %all_gather.3 = bf16[1,128,2048]{2,1,0:T(8,128)(2,1)S(1)} all-gather(bf16[1,8,2048]{2,1,0:T(8,128)(2,1)} %param.14), channel_id=1, replica_groups=mesh['row'=32,'col'=16] {'col'}, dimensions={1}, use_global_device_ids=true | all-gather | bytes 557056 | tf_op jit(solution)/shard_map/all_gather | solution.py:51
  63.3 1.1 copy.115
  65.3 1.0 copy.94
  66.2 1.0 copy.99
  68.0 3.6 %collective-permute-start.12 = (bf16[1,1,1,32,2048]{4,3,2,1,0:T(8,128)(2,1)}, bf16[1,1,1,32,2048]{4,3,2,1,0:T(8,128)(2,1)S(1)}, u32[]{:S(2)}, u32[]{:S(2)}) collective-permute-start(bf16[1,1,1,32,2048]{4,3,2,1,0:T(8,128)(2,1)} %bitcast.222), channel_id=1, source_target_pairs={{0,16},{16,32},{32,48},{48,64},{64,80},{80,96},{96,112},{112,128},... | collective-permute-start | bytes 393224 | tf_op jit(solution)/shard_map/ppermute | solution.py:16
  71.7 4.0 %collective-permute-start.8 = (bf16[1,1,2,64,2048]{4,3,2,1,0:T(8,128)(2,1)}, bf16[1,1,2,64,2048]{4,3,2,1,0:T(8,128)(2,1)S(1)}, u32[]{:S(2)}, u32[]{:S(2)}) collective-permute-start(bf16[1,1,2,64,2048]{4,3,2,1,0:T(8,128)(2,1)} %param.9), channel_id=1, source_target_pairs={{0,16},{16,32},{32,48},{48,64},{64,80},{80,96},{96,112},{112,128},... | collective-permute-start | bytes 1572872 | tf_op jit(solution)/shard_map/ppermute | solution.py:16
  75.6 1.0 pad_maximum_fusion.3
  76.6 1.3 collective-permute-start.9
  77.9 8.9 %collective-permute-start.7 = (bf16[1,3,1,32,2048]{4,3,2,1,0:T(8,128)(2,1)S(1)}, bf16[1,3,1,32,2048]{4,3,2,1,0:T(8,128)(2,1)S(1)}, u32[]{:S(2)}, u32[]{:S(2)}) collective-permute-start(bf16[1,3,1,32,2048]{4,3,2,1,0:T(8,128)(2,1)S(1)} %pad_maximum_fusion.3), channel_id=1, source_target_pairs={{1,0},{2,1},{3,2},{4,3},{5,4},{6,5},{7,6},{8,7},{9,8},{10,9},{11,1... | collective-permute-start | bytes 1179656 | tf_op jit(solution)/shard_map/ppermute | solution.py:19
  87.6 1.9 collective-permute-start.6
  89.7 8.4 %collective-permute-start.15 = (bf16[1,3,1,32,2048]{4,3,2,1,0:T(8,128)(2,1)}, bf16[1,3,1,32,2048]{4,3,2,1,0:T(8,128)(2,1)}, u32[]{:S(2)}, u32[]{:S(2)}) collective-permute-start(bf16[1,3,1,32,2048]{4,3,2,1,0:T(8,128)(2,1)} %pad_maximum_fusion.2), channel_id=1, source_target_pairs={{1,0},{2,1},{3,2},{4,3},{5,4},{6,5},{7,6},{8,7},{9,8},{10,9},{11,1... | collective-permute-start | bytes 1179656 | tf_op jit(solution)/shard_map/ppermute | solution.py:19
  98.2 1.1 constant_dynamic-update-slice_fusion.1
  99.3 1.9 collective-permute-start.14
  101.2 1.1 constant_dynamic-update-slice_fusion.3
  102.3 1.2 fusion.21
  103.6 8.4 %collective-permute-start.3 = (bf16[1,3,1,64,2048]{4,3,2,1,0:T(8,128)(2,1)}, bf16[1,3,1,64,2048]{4,3,2,1,0:T(8,128)(2,1)}, u32[]{:S(2)}, u32[]{:S(2)}) collective-permute-start(bf16[1,3,1,64,2048]{4,3,2,1,0:T(8,128)(2,1)} %get-tuple-element.59), channel_id=1, source_target_pairs={{1,0},{2,1},{3,2},{4,3},{5,4},{6,5},{7,6},{8,7},{9,8},{10,9},{11,1... | collective-permute-start | bytes 2359304 | tf_op jit(solution)/shard_map/ppermute | solution.py:19
  112.1 1.3 fusion.20
  113.4 11.0 %collective-permute-done.7 = bf16[1,3,1,32,2048]{4,3,2,1,0:T(8,128)(2,1)S(1)} collective-permute-done((bf16[1,3,1,32,2048]{4,3,2,1,0:T(8,128)(2,1)S(1)}, bf16[1,3,1,32,2048]{4,3,2,1,0:T(8,128)(2,1)S(1)}, u32[]{:S(2)}, u32[]{:S(2)}) %collective-permute-start.7) | collective-permute-done | bytes 393248 | tf_op jit(solution)/shard_map/ppermute | solution.py:19
  124.4 4.9 %collective-permute-start.2 = (bf16[1,3,1,64,2048]{4,3,2,1,0:T(8,128)(2,1)}, bf16[1,3,1,64,2048]{4,3,2,1,0:T(8,128)(2,1)}, u32[]{:S(2)}, u32[]{:S(2)}) collective-permute-start(bf16[1,3,1,64,2048]{4,3,2,1,0:T(8,128)(2,1)} %get-tuple-element.58), channel_id=1, source_target_pairs={{0,1},{1,2},{2,3},{3,4},{4,5},{5,6},{6,7},{7,8},{8,9},{9,10},{10,1... | collective-permute-start | bytes 2359304 | tf_op jit(solution)/shard_map/ppermute | solution.py:16
  129.3 1.2 pad_maximum_fusion.1
  130.4 2.9 %gather_fusion = bf16[16,16,2048]{2,1,0:T(8,128)(2,1)} fusion(bf16[18,16,2048]{2,1,0:T(8,128)(2,1)} %bitcast.172, s32[1024]{0:T(1024)S(1)} %pad_clamp_fusion), kind=kCustom, calls=%fused_computation | custom fusion | bytes 2097216 | tf_op jit(solution)/shard_map/while/body/eval_jaxpr/gather | solution.py:95
  133.3 2.5 %copy.126 = bf16[32,8,16,128]{3,2,1,0:T(8,128)(2,1)} copy(bf16[32,8,16,128]{3,1,2,0:T(8,128)(2,1)} %bitcast.176) | data formatting | bytes 2097152
  135.8 5.8 %collective-permute-start.11 = (bf16[1,3,1,64,2048]{4,3,2,1,0:T(8,128)(2,1)}, bf16[1,3,1,64,2048]{4,3,2,1,0:T(8,128)(2,1)}, u32[]{:S(2)}, u32[]{:S(2)}) collective-permute-start(bf16[1,3,1,64,2048]{4,3,2,1,0:T(8,128)(2,1)} %get-tuple-element.57), channel_id=1, source_target_pairs={{1,0},{2,1},{3,2},{4,3},{5,4},{6,5},{7,6},{8,7},{9,8},{10,9},{11,1... | collective-permute-start | bytes 2359304 | tf_op jit(solution)/shard_map/ppermute | solution.py:19
  141.6 1.9 collective-permute-start.10
  144.2 2.3 %pad_maximum_fusion = bf16[1,3,3,32,2048]{4,3,2,1,0:T(8,128)(2,1)} fusion(bf16[1,3,1,32,2048]{4,3,2,1,0:T(8,128)(2,1)} %collective-permute-done.15, bf16[1,1,1,32,2048]{4,3,2,1,0:T(8,128)(2,1)S(1)} %collective-permute-done.13, bf16[1,1,1,32,2048]{4,3,2,1,0:T(8,128)(2,1)S(1)} %bitcast.224, bf16[1,1,1,32,2048]{4,3,2,1,0:T(8,128)(2,1)} %copy-done.10, ...), kind=kLoop, calls=%fused_computation.16 | loop fusion | flops 2359296 | bytes 2359296 | tf_op jit(solution)/shard_map/concatenate | solution.py:20
  146.5 2.9 %gather_fusion.1 = bf16[16,16,2048]{2,1,0:T(8,128)(2,1)} fusion(bf16[18,16,2048]{2,1,0:T(8,128)(2,1)} %bitcast.171, s32[1024]{0:T(1024)S(1)} %pad_clamp_fusion), kind=kCustom, calls=%fused_computation.1 | custom fusion | bytes 2097216 | tf_op jit(solution)/shard_map/while/body/eval_jaxpr/gather | solution.py:94
  149.4 2.4 %copy.114 = bf16[32,8,16,128]{3,2,1,0:T(8,128)(2,1)} copy(bf16[32,8,16,128]{3,1,2,0:T(8,128)(2,1)} %bitcast.175) | data formatting | bytes 2097152
  151.8 1.1 copy.116
  152.9 1.5 fusion.10
  154.8 6.7 %collective-permute-done.3 = bf16[1,3,1,64,2048]{4,3,2,1,0:T(8,128)(2,1)} collective-permute-done((bf16[1,3,1,64,2048]{4,3,2,1,0:T(8,128)(2,1)}, bf16[1,3,1,64,2048]{4,3,2,1,0:T(8,128)(2,1)}, u32[]{:S(2)}, u32[]{:S(2)}) %collective-permute-start.3) | collective-permute-done | bytes 786464 | tf_op jit(solution)/shard_map/ppermute | solution.py:19
  161.5 16.6 %collective-permute-done.2 = bf16[1,3,1,64,2048]{4,3,2,1,0:T(8,128)(2,1)} collective-permute-done((bf16[1,3,1,64,2048]{4,3,2,1,0:T(8,128)(2,1)}, bf16[1,3,1,64,2048]{4,3,2,1,0:T(8,128)(2,1)}, u32[]{:S(2)}, u32[]{:S(2)}) %collective-permute-start.2) | collective-permute-done | bytes 786464 | tf_op jit(solution)/shard_map/ppermute | solution.py:16
  178.1 1.7 maximum_bitcast_fusion.1
  181.5 1.0 copy_dynamic-update-slice_fusion.19
  182.5 6.1 %collective-permute-done.11 = bf16[1,3,1,64,2048]{4,3,2,1,0:T(8,128)(2,1)} collective-permute-done((bf16[1,3,1,64,2048]{4,3,2,1,0:T(8,128)(2,1)}, bf16[1,3,1,64,2048]{4,3,2,1,0:T(8,128)(2,1)}, u32[]{:S(2)}, u32[]{:S(2)}) %collective-permute-start.11) | collective-permute-done | bytes 786464 | tf_op jit(solution)/shard_map/ppermute | solution.py:19
  188.6 15.1 %collective-permute-done.10 = bf16[1,3,1,64,2048]{4,3,2,1,0:T(8,128)(2,1)} collective-permute-done((bf16[1,3,1,64,2048]{4,3,2,1,0:T(8,128)(2,1)}, bf16[1,3,1,64,2048]{4,3,2,1,0:T(8,128)(2,1)}, u32[]{:S(2)}, u32[]{:S(2)}) %collective-permute-start.10) | collective-permute-done | bytes 786464 | tf_op jit(solution)/shard_map/ppermute | solution.py:16
  203.7 1.7 maximum_bitcast_fusion
  209.3 2.3 %bitcast_reduce_fusion = (f32[2,16,64]{2,1,0:T(8,128)S(1)}, f32[2,16,704,64]{2,3,1,0:T(8,128)S(1)}) fusion(pred[2,704]{1,0:T(4,128)(4,1)S(1)} %concatenate.92, bf16[2,704,16,128]{3,1,2,0:T(8,128)(2,1)S(1)} %copy_dynamic-update-slice_fusion, bf16[2,64,16,128]{3,2,1,0:T(8,128)(2,1)S(1)} %bitcast.170), kind=kOutput, calls=%fused_computation.3 | convolution fusion | flops 373422080 | bytes 12068224 | tf_op jit(solution)/shard_map/while/body/eval_jaxpr/bqhd,bkhd->bhqk/dot_general | solution.py:101
  211.7 1.9 fusion.1
  216.1 2.2 fusion.4
  218.3 1.0 fusion.6
  219.6 1.0 convert_element_type.27
  (109 shorter events, 12.4 us)
Async XLA Ops:
  0.0 89.6 %copy-start.4 = (bf16[1,1,2,64,2048]{4,3,2,1,0:T(8,128)(2,1)S(1)}, bf16[1,1,2,64,2048]{4,3,2,1,0:T(8,128)(2,1)}, u32[]{:S(2)}) copy-start(bf16[1,1,2,64,2048]{4,3,2,1,0:T(8,128)(2,1)} %param.10) | copy-start | bytes 1572868
  0.0 86.8 %copy-start.7 = (bf16[2,16,2048]{2,1,0:T(8,128)(2,1)S(1)}, bf16[2,16,2048]{2,1,0:T(8,128)(2,1)}, u32[]{:S(2)}) copy-start(bf16[2,16,2048]{2,1,0:T(8,128)(2,1)} %param.11) | copy-start | bytes 393220
  0.0 87.6 %collective-permute-start = (bf16[1,1,2,64,2048]{4,3,2,1,0:T(8,128)(2,1)}, bf16[1,1,2,64,2048]{4,3,2,1,0:T(8,128)(2,1)S(1)}, u32[]{:S(2)}, u32[]{:S(2)}) collective-permute-start(bf16[1,1,2,64,2048]{4,3,2,1,0:T(8,128)(2,1)} %param.10), channel_id=1, source_target_pairs={{0,16},{16,32},{32,48},{48,64},{64,80},{80,96},{96,112},{112,128},... | collective-permute-start | bytes 1572872 | tf_op jit(solution)/shard_map/ppermute | solution.py:16
  3.6 95.7 %collective-permute-start.1 = (bf16[1,1,2,64,2048]{4,3,2,1,0:T(8,128)(2,1)}, bf16[1,1,2,64,2048]{4,3,2,1,0:T(8,128)(2,1)}, u32[]{:S(2)}, u32[]{:S(2)}) collective-permute-start(bf16[1,1,2,64,2048]{4,3,2,1,0:T(8,128)(2,1)} %param.10), channel_id=1, source_target_pairs={{16,0},{32,16},{48,32},{64,48},{80,64},{96,80},{112,96},{128,112},... | collective-permute-start | bytes 1572872 | tf_op jit(solution)/shard_map/ppermute | solution.py:19
  4.9 63.1 %collective-permute-start.5 = (bf16[1,1,1,32,2048]{4,3,2,1,0:T(8,128)(2,1)}, bf16[1,1,1,32,2048]{4,3,2,1,0:T(8,128)(2,1)S(1)}, u32[]{:S(2)}, u32[]{:S(2)}) collective-permute-start(bf16[1,1,1,32,2048]{4,3,2,1,0:T(8,128)(2,1)} %bitcast.217), channel_id=1, source_target_pairs={{16,0},{32,16},{48,32},{64,48},{80,64},{96,80},{112,96},{128,112},... | collective-permute-start | bytes 393224 | tf_op jit(solution)/shard_map/ppermute | solution.py:19
  6.2 65.4 %collective-permute-start.4 = (bf16[1,1,1,32,2048]{4,3,2,1,0:T(8,128)(2,1)}, bf16[1,1,1,32,2048]{4,3,2,1,0:T(8,128)(2,1)S(1)}, u32[]{:S(2)}, u32[]{:S(2)}) collective-permute-start(bf16[1,1,1,32,2048]{4,3,2,1,0:T(8,128)(2,1)} %bitcast.218), channel_id=1, source_target_pairs={{0,16},{16,32},{32,48},{48,64},{64,80},{80,96},{96,112},{112,128},... | collective-permute-start | bytes 393224 | tf_op jit(solution)/shard_map/ppermute | solution.py:16
  11.4 65.2 %collective-permute-start.13 = (bf16[1,1,1,32,2048]{4,3,2,1,0:T(8,128)(2,1)}, bf16[1,1,1,32,2048]{4,3,2,1,0:T(8,128)(2,1)S(1)}, u32[]{:S(2)}, u32[]{:S(2)}) collective-permute-start(bf16[1,1,1,32,2048]{4,3,2,1,0:T(8,128)(2,1)} %bitcast.221), channel_id=1, source_target_pairs={{16,0},{32,16},{48,32},{64,48},{80,64},{96,80},{112,96},{128,112},... | collective-permute-start | bytes 393224 | tf_op jit(solution)/shard_map/ppermute | solution.py:19
  14.4 137.4 %all-to-all-start = ((bf16[16,1,8,2048]{3,2,1,0:T(8,128)(2,1)}), bf16[16,1,8,2048]{3,2,1,0:T(8,128)(2,1)}, u32[]{:S(2)}, u32[]{:S(2)}) async-start(bf16[16,1,8,2048]{3,2,1,0:T(8,128)(2,1)} %stack.2), calls=%async_computation | async-start | bytes 1048576 | tf_op jit(solution)/shard_map/all_to_all | solution.py:49
  64.5 0.8 copy-start
  68.0 9.9 %collective-permute-start.12 = (bf16[1,1,1,32,2048]{4,3,2,1,0:T(8,128)(2,1)}, bf16[1,1,1,32,2048]{4,3,2,1,0:T(8,128)(2,1)S(1)}, u32[]{:S(2)}, u32[]{:S(2)}) collective-permute-start(bf16[1,1,1,32,2048]{4,3,2,1,0:T(8,128)(2,1)} %bitcast.222), channel_id=1, source_target_pairs={{0,16},{16,32},{32,48},{48,64},{64,80},{80,96},{96,112},{112,128},... | collective-permute-start | bytes 393224 | tf_op jit(solution)/shard_map/ppermute | solution.py:16
  71.7 18.0 %copy-start.8 = (bf16[1,1,1,32,2048]{4,3,2,1,0:T(8,128)(2,1)}, bf16[1,1,1,32,2048]{4,3,2,1,0:T(8,128)(2,1)S(1)}, u32[]{:S(2)}) copy-start(bf16[1,1,1,32,2048]{4,3,2,1,0:T(8,128)(2,1)S(1)} %collective-permute-done.4) | copy-start | bytes 393220
  71.7 18.0 %collective-permute-start.8 = (bf16[1,1,2,64,2048]{4,3,2,1,0:T(8,128)(2,1)}, bf16[1,1,2,64,2048]{4,3,2,1,0:T(8,128)(2,1)S(1)}, u32[]{:S(2)}, u32[]{:S(2)}) collective-permute-start(bf16[1,1,2,64,2048]{4,3,2,1,0:T(8,128)(2,1)} %param.9), channel_id=1, source_target_pairs={{0,16},{16,32},{32,48},{48,64},{64,80},{80,96},{96,112},{112,128},... | collective-permute-start | bytes 1572872 | tf_op jit(solution)/shard_map/ppermute | solution.py:16
  76.6 27.0 %collective-permute-start.9 = (bf16[1,1,2,64,2048]{4,3,2,1,0:T(8,128)(2,1)}, bf16[1,1,2,64,2048]{4,3,2,1,0:T(8,128)(2,1)S(1)}, u32[]{:S(2)}, u32[]{:S(2)}) collective-permute-start(bf16[1,1,2,64,2048]{4,3,2,1,0:T(8,128)(2,1)} %param.9), channel_id=1, source_target_pairs={{16,0},{32,16},{48,32},{64,48},{80,64},{96,80},{112,96},{128,112},... | collective-permute-start | bytes 1572872 | tf_op jit(solution)/shard_map/ppermute | solution.py:19
  77.9 11.7 %copy-start.10 = (bf16[1,1,1,32,2048]{4,3,2,1,0:T(8,128)(2,1)}, bf16[1,1,1,32,2048]{4,3,2,1,0:T(8,128)(2,1)S(1)}, u32[]{:S(2)}) copy-start(bf16[1,1,1,32,2048]{4,3,2,1,0:T(8,128)(2,1)S(1)} %collective-permute-done.12) | copy-start | bytes 393220
  77.9 46.5 %collective-permute-start.7 = (bf16[1,3,1,32,2048]{4,3,2,1,0:T(8,128)(2,1)S(1)}, bf16[1,3,1,32,2048]{4,3,2,1,0:T(8,128)(2,1)S(1)}, u32[]{:S(2)}, u32[]{:S(2)}) collective-permute-start(bf16[1,3,1,32,2048]{4,3,2,1,0:T(8,128)(2,1)S(1)} %pad_maximum_fusion.3), channel_id=1, source_target_pairs={{1,0},{2,1},{3,2},{4,3},{5,4},{6,5},{7,6},{8,7},{9,8},{10,9},{11,1... | collective-permute-start | bytes 1179656 | tf_op jit(solution)/shard_map/ppermute | solution.py:19
  87.6 41.6 %collective-permute-start.6 = (bf16[1,3,1,32,2048]{4,3,2,1,0:T(8,128)(2,1)S(1)}, bf16[1,3,1,32,2048]{4,3,2,1,0:T(8,128)(2,1)S(1)}, u32[]{:S(2)}, u32[]{:S(2)}) collective-permute-start(bf16[1,3,1,32,2048]{4,3,2,1,0:T(8,128)(2,1)S(1)} %pad_maximum_fusion.3), channel_id=1, source_target_pairs={{0,1},{1,2},{2,3},{3,4},{4,5},{5,6},{6,7},{7,8},{8,9},{9,10},{10,1... | collective-permute-start | bytes 1179656 | tf_op jit(solution)/shard_map/ppermute | solution.py:16
  89.6 39.7 %copy-start.6 = (bf16[2,16,2048]{2,1,0:T(8,128)(2,1)S(1)}, bf16[2,16,2048]{2,1,0:T(8,128)(2,1)}, u32[]{:S(2)}) copy-start(bf16[2,16,2048]{2,1,0:T(8,128)(2,1)} %param.12) | copy-start | bytes 393220
  89.7 51.9 %collective-permute-start.15 = (bf16[1,3,1,32,2048]{4,3,2,1,0:T(8,128)(2,1)}, bf16[1,3,1,32,2048]{4,3,2,1,0:T(8,128)(2,1)}, u32[]{:S(2)}, u32[]{:S(2)}) collective-permute-start(bf16[1,3,1,32,2048]{4,3,2,1,0:T(8,128)(2,1)} %pad_maximum_fusion.2), channel_id=1, source_target_pairs={{1,0},{2,1},{3,2},{4,3},{5,4},{6,5},{7,6},{8,7},{9,8},{10,9},{11,1... | collective-permute-start | bytes 1179656 | tf_op jit(solution)/shard_map/ppermute | solution.py:19
  98.1 31.1 %copy-start.9 = (bf16[1,1,1,32,2048]{4,3,2,1,0:T(8,128)(2,1)S(1)}, bf16[1,1,1,32,2048]{4,3,2,1,0:T(8,128)(2,1)}, u32[]{:S(2)}) copy-start(bf16[1,1,1,32,2048]{4,3,2,1,0:T(8,128)(2,1)} %copy-done.8) | copy-start | bytes 393220
  99.3 44.8 %collective-permute-start.14 = (bf16[1,3,1,32,2048]{4,3,2,1,0:T(8,128)(2,1)}, bf16[1,3,1,32,2048]{4,3,2,1,0:T(8,128)(2,1)}, u32[]{:S(2)}, u32[]{:S(2)}) collective-permute-start(bf16[1,3,1,32,2048]{4,3,2,1,0:T(8,128)(2,1)} %pad_maximum_fusion.2), channel_id=1, source_target_pairs={{0,1},{1,2},{2,3},{3,4},{4,5},{5,6},{6,7},{7,8},{8,9},{9,10},{10,1... | collective-permute-start | bytes 1179656 | tf_op jit(solution)/shard_map/ppermute | solution.py:16
  103.6 57.9 %collective-permute-start.3 = (bf16[1,3,1,64,2048]{4,3,2,1,0:T(8,128)(2,1)}, bf16[1,3,1,64,2048]{4,3,2,1,0:T(8,128)(2,1)}, u32[]{:S(2)}, u32[]{:S(2)}) collective-permute-start(bf16[1,3,1,64,2048]{4,3,2,1,0:T(8,128)(2,1)} %get-tuple-element.59), channel_id=1, source_target_pairs={{1,0},{2,1},{3,2},{4,3},{5,4},{6,5},{7,6},{8,7},{9,8},{10,9},{11,1... | collective-permute-start | bytes 2359304 | tf_op jit(solution)/shard_map/ppermute | solution.py:19
  124.4 53.7 %collective-permute-start.2 = (bf16[1,3,1,64,2048]{4,3,2,1,0:T(8,128)(2,1)}, bf16[1,3,1,64,2048]{4,3,2,1,0:T(8,128)(2,1)}, u32[]{:S(2)}, u32[]{:S(2)}) collective-permute-start(bf16[1,3,1,64,2048]{4,3,2,1,0:T(8,128)(2,1)} %get-tuple-element.58), channel_id=1, source_target_pairs={{0,1},{1,2},{2,3},{3,4},{4,5},{5,6},{6,7},{7,8},{8,9},{9,10},{10,1... | collective-permute-start | bytes 2359304 | tf_op jit(solution)/shard_map/ppermute | solution.py:16
  135.8 52.8 %collective-permute-start.11 = (bf16[1,3,1,64,2048]{4,3,2,1,0:T(8,128)(2,1)}, bf16[1,3,1,64,2048]{4,3,2,1,0:T(8,128)(2,1)}, u32[]{:S(2)}, u32[]{:S(2)}) collective-permute-start(bf16[1,3,1,64,2048]{4,3,2,1,0:T(8,128)(2,1)} %get-tuple-element.57), channel_id=1, source_target_pairs={{1,0},{2,1},{3,2},{4,3},{5,4},{6,5},{7,6},{8,7},{9,8},{10,9},{11,1... | collective-permute-start | bytes 2359304 | tf_op jit(solution)/shard_map/ppermute | solution.py:19
  141.6 62.1 %collective-permute-start.10 = (bf16[1,3,1,64,2048]{4,3,2,1,0:T(8,128)(2,1)}, bf16[1,3,1,64,2048]{4,3,2,1,0:T(8,128)(2,1)}, u32[]{:S(2)}, u32[]{:S(2)}) collective-permute-start(bf16[1,3,1,64,2048]{4,3,2,1,0:T(8,128)(2,1)} %get-tuple-element.56), channel_id=1, source_target_pairs={{0,1},{1,2},{2,3},{3,4},{4,5},{5,6},{6,7},{7,8},{8,9},{9,10},{10,1... | collective-permute-start | bytes 2359304 | tf_op jit(solution)/shard_map/ppermute | solution.py:16
  207.1 1.8 copy-start.3
  207.3 1.9 copy-start.1
  208.9 5.4 %slice-start = ((s8[5767168]{0:T(1024)(128)(4,1)}), s8[4194304]{0:T(1024)(128)(4,1)S(1)}, s32[]{:S(2)}) async-start(s8[5767168]{0:T(1024)(128)(4,1)} %bitcast.225), calls=%async_computation.1 | async-start | bytes 8388608
  209.3 5.0 %slice-start.1 = ((s8[5767168]{0:T(1024)(128)(4,1)}), s8[1572864]{0:T(1024)(128)(4,1)S(1)}, s32[]{:S(2)}) async-start(s8[5767168]{0:T(1024)(128)(4,1)} %bitcast.225), calls=%async_computation.2 | async-start | bytes 3145728
  213.5 2.2 copy-start.2
  216.1 2.2 copy-start.5
